TPU v7x, 256 devices: a whole 4x4x8 slice. The times are simulated.
256 devices in a mesh: blk: 32 (over x, z), uly: 8 (over y, core).
Axes of the slice: x: 4, y: 4, z: 8, core: 2. Of those that a mesh axis runs over, the one named last changes fastest.
Arguments:
- tokens: bfloat16 [12288, 3072], P(('blk', 'uly')), may hold values from -6 to 6
- mod_shift: float32 [3072], replicated, may hold values from -3 to 3
- mod_scale: float32 [3072], replicated, may hold values from -2 to 6
- out_gate: float32 [3072], replicated, may hold values from 0.5 to 1.5
- w_qkv: bfloat16 [3072, 24, 384], P(None, 'uly'), may hold values from -0.109375 to 0.109375
- w_out: bfloat16 [3072, 3072], P('uly'), may hold values from -0.109375 to 0.109375
- tile_map: int32 [32], replicated, may hold values from 0 to 31, as said below
- window_corner: int32 [32, 2], replicated, may hold values from 0 to 5, as said below
Outputs:
- mixed: bfloat16 [12288, 3072], P(('blk', 'uly'))
Inputs may be any that keep to these rules, and one draw needn't show every extreme that they name: `tile_map`: A permutation of the tile positions; position j holds a grid tile whose number differs from j by at most 1. `window_corner`: each query tile's 3 x 3 window lies inside the grid and contains the grid tile that its own position holds.
All inputs are finite; a program needn't handle non-finite values.
Results may differ from a plain program's by a relative error of at most 0.02.
The roundings to bfloat16 on the way count: a program that leaves them out, or rounds other values in their place, can miss the bound.
Values may be sent and summed in bfloat16 or wider, within the bound.
A program may use at most 128 MiB of HBM per device.

v0:
```python
import jax
import jax.numpy as jnp
from jax import lax
from jax.sharding import PartitionSpec as P

TILE = 384
WIN = 3
GW = 4


def from_behind(block, axis, distance):
    devices = range(lax.axis_size(axis))
    route = [(i - distance, i) for i in devices if i - distance in devices]
    return lax.ppermute(block, axis, route)


def on_device(tokens, mod_shift, mod_scale, out_gate, w_qkv, w_out, tile_map, window_corner):
    values_in = tokens.astype(jnp.float32)
    mean_row = jnp.mean(values_in, axis=-1, keepdims=True)
    centred = values_in - mean_row
    variance = jnp.mean(centred * centred, axis=-1, keepdims=True)
    normed = (centred * lax.rsqrt(variance + 1e-06) * (1.0 + mod_scale) + mod_shift).astype(
        jnp.bfloat16
    )
    heads_dev = w_qkv.shape[1]
    head_dim = w_qkv.shape[2] // 3
    qkv = jnp.einsum(
        "td,dhe->the",
        lax.all_gather(normed, "uly", axis=0, tiled=True),
        w_qkv,
        preferred_element_type=jnp.float32,
    ).astype(jnp.bfloat16)
    group_rows = qkv.shape[0]
    tiles_here = group_rows // TILE
    all_tiles = tile_map.shape[0]
    queries = qkv[:, :, :head_dim]
    keyval = qkv[:, :, head_dim:]
    shard_idx = lax.axis_index("blk")
    n_blk = lax.axis_size("blk")
    first_tile = shard_idx * tiles_here
    query_corner = lax.dynamic_slice(window_corner, (first_tile, 0), (tiles_here, 2))
    softmax_factor = 1.0 / jnp.sqrt(jnp.float32(head_dim))

    def attend(running, kv_tile, key_tile, is_valid):
        safe_tile = jnp.clip(key_tile, 0, all_tiles - 1)
        key_grid = lax.dynamic_index_in_dim(tile_map, safe_tile, keepdims=False)
        row_gap = key_grid // GW - query_corner[:, 0]
        col_gap = key_grid % GW - query_corner[:, 1]
        inside = (row_gap >= 0) & (row_gap < WIN) & (col_gap >= 0) & (col_gap < WIN) & is_valid

        def compute(state):
            highest, total, accum = state
            row_ok = jnp.repeat(inside, TILE)[None, :, None]
            scores = (
                jnp.einsum(
                    "qhd,khd->hqk",
                    queries,
                    kv_tile[:, :, :head_dim],
                    preferred_element_type=jnp.float32,
                )
                * softmax_factor
            )
            scores = jnp.where(row_ok, scores, -1e30)
            new_high = jnp.maximum(highest, jnp.max(scores, axis=-1))
            probs = jnp.where(row_ok, jnp.exp(scores - new_high[:, :, None]), 0.0)
            factor = jnp.exp(highest - new_high)
            total = total * factor + jnp.sum(probs, axis=-1)
            weights = probs.astype(jnp.bfloat16)
            accum = accum * factor[:, :, None] + jnp.einsum(
                "hqk,khd->hqd",
                weights,
                kv_tile[:, :, head_dim:],
                preferred_element_type=jnp.float32,
            )
            return (new_high, total, accum)

        def keep(state):
            return state

        return lax.cond(jnp.any(inside), compute, keep, running)

    def attend_group(running, arrived, source):
        is_valid = (source >= 0) & (source < n_blk)
        running = attend(running, arrived, source * tiles_here + 0, is_valid)
        return running

    running = (
        jnp.full((heads_dev, group_rows), -1e30, jnp.float32),
        jnp.zeros((heads_dev, group_rows), jnp.float32),
        jnp.zeros((heads_dev, group_rows, head_dim), jnp.float32),
    )
    reach = min((2 * GW + 3 + tiles_here) // tiles_here, n_blk - 1)
    running = attend_group(running, keyval, shard_idx)
    for offset in range(-reach, reach + 1):
        if offset != 0:
            arrived = from_behind(keyval, "blk", offset)
            running = attend_group(running, arrived, shard_idx - offset)
    highest, total, accum = running
    attn = (accum / total[:, :, None]).astype(jnp.bfloat16)
    attn = jnp.transpose(attn, (1, 0, 2)).reshape(group_rows, heads_dev * head_dim)
    summed = lax.psum_scatter(
        jnp.dot(attn, w_out, preferred_element_type=jnp.float32).astype(jnp.bfloat16),
        "uly",
        scatter_dimension=0,
        tiled=True,
    ).astype(jnp.float32)
    return (out_gate * summed).astype(jnp.bfloat16)


def solution(mesh):
    in_specs = (
        P(("blk", "uly"), None),
        P(),
        P(),
        P(),
        P(None, "uly", None),
        P("uly", None),
        P(),
        P(),
    )
    out_specs = P(("blk", "uly"), None)
    return jax.shard_map(
        on_device, mesh=mesh, in_specs=in_specs, out_specs=out_specs, check_vma=False
    )
```

profile of v0, /device:TPU:4, one launch (start us, length us, event | category | flops | bytes accessed | tf_op | source)
XLA Modules:
  0.0 685.6 jit_solution(6186179026058369950)
XLA Ops:
  9.7 1.9 fusion.386
  11.7 31.2 %all-gather.2.cloned.1.call-done = bf16[384,3072]{1,0:T(8,128)(2,1)} async-done(((bf16[48,3072]{1,0:T(8,128)(2,1)}), bf16[384,3072]{1,0:T(8,128)(2,1)}) %all-gather.2.cloned.1.call-update) | async-done | bytes 2359312 | tf_op jit(solution)/shard_map/all_gather | solution.py:29
  42.9 6.9 %fusion.378 = bf16[384,3,384]{2,0,1:T(8,128)(2,1)S(1)} fusion(bf16[3072,3,384]{2,0,1:T(8,128)(2,1)} %param.62, bf16[384,3072]{1,0:T(8,128)(2,1)} %all-gather.2.cloned.1.call-done), kind=kOutput, calls=%fused_computation.479 | convolution fusion | flops 2718351360 | bytes 10321920 | tf_op jit(solution)/shard_map/td,dhe->the/dot_general | solution.py:27
  51.6 7.6 %collective-permute-start = (bf16[384,3,256]{2,0,1:T(8,128)(2,1)}, bf16[384,3,256]{2,0,1:T(8,128)(2,1)}, u32[]{:S(2)}, u32[]{:S(2)}) collective-permute-start(bf16[384,3,256]{2,0,1:T(8,128)(2,1)} %slice.214), channel_id=1, source_target_pairs={{96,0},{104,8},{112,16},{120,24},{128,32},{136,40},{144,48},{152,5... | collective-permute-start | bytes 1769480 | tf_op jit(solution)/shard_map/ppermute | solution.py:14
  59.2 1.9 collective-permute-start.1
  61.2 1.9 collective-permute-start.2
  63.1 1.9 collective-permute-start.3
  65.0 1.9 collective-permute-start.4
  67.0 18.3 %collective-permute-done = bf16[384,3,256]{2,0,1:T(8,128)(2,1)} collective-permute-done((bf16[384,3,256]{2,0,1:T(8,128)(2,1)}, bf16[384,3,256]{2,0,1:T(8,128)(2,1)}, u32[]{:S(2)}, u32[]{:S(2)}) %collective-permute-start) | collective-permute-done | bytes 589856 | tf_op jit(solution)/shard_map/ppermute | solution.py:14
  85.3 6.3 collective-permute-start.5
  91.6 34.4 %collective-permute-done.1 = bf16[384,3,256]{2,0,1:T(8,128)(2,1)} collective-permute-done((bf16[384,3,256]{2,0,1:T(8,128)(2,1)}, bf16[384,3,256]{2,0,1:T(8,128)(2,1)}, u32[]{:S(2)}, u32[]{:S(2)}) %collective-permute-start.1) | collective-permute-done | bytes 589856 | tf_op jit(solution)/shard_map/ppermute | solution.py:14
  126.0 1.9 collective-permute-start.6
  127.9 23.2 %collective-permute-done.2 = bf16[384,3,256]{2,0,1:T(8,128)(2,1)} collective-permute-done((bf16[384,3,256]{2,0,1:T(8,128)(2,1)}, bf16[384,3,256]{2,0,1:T(8,128)(2,1)}, u32[]{:S(2)}, u32[]{:S(2)}) %collective-permute-start.2) | collective-permute-done | bytes 589856 | tf_op jit(solution)/shard_map/ppermute | solution.py:14
  151.1 1.9 collective-permute-start.7
  153.0 12.4 %collective-permute-done.3 = bf16[384,3,256]{2,0,1:T(8,128)(2,1)} collective-permute-done((bf16[384,3,256]{2,0,1:T(8,128)(2,1)}, bf16[384,3,256]{2,0,1:T(8,128)(2,1)}, u32[]{:S(2)}, u32[]{:S(2)}) %collective-permute-start.3) | collective-permute-done | bytes 589856 | tf_op jit(solution)/shard_map/ppermute | solution.py:14
  165.4 7.0 %collective-permute-start.8 = (bf16[384,3,256]{2,0,1:T(8,128)(2,1)}, bf16[384,3,256]{2,0,1:T(8,128)(2,1)}, u32[]{:S(2)}, u32[]{:S(2)}) collective-permute-start(bf16[384,3,256]{2,0,1:T(8,128)(2,1)} %slice.214), channel_id=1, source_target_pairs={{32,0},{40,8},{48,16},{56,24},{64,32},{72,40},{80,48},{88,56},{96,... | collective-permute-start | bytes 1769480 | tf_op jit(solution)/shard_map/ppermute | solution.py:14
  172.4 17.0 %collective-permute-start.9 = (bf16[384,3,256]{2,0,1:T(8,128)(2,1)}, bf16[384,3,256]{2,0,1:T(8,128)(2,1)}, u32[]{:S(2)}, u32[]{:S(2)}) collective-permute-start(bf16[384,3,256]{2,0,1:T(8,128)(2,1)} %slice.214), channel_id=1, source_target_pairs={{24,0},{32,8},{40,16},{48,24},{56,32},{64,40},{72,48},{80,56},{88,... | collective-permute-start | bytes 1769480 | tf_op jit(solution)/shard_map/ppermute | solution.py:14
  189.4 1.9 collective-permute-start.10
  191.4 2.5 collective-permute-start.11
  193.9 23.3 %collective-permute-done.7 = bf16[384,3,256]{2,0,1:T(8,128)(2,1)} collective-permute-done((bf16[384,3,256]{2,0,1:T(8,128)(2,1)}, bf16[384,3,256]{2,0,1:T(8,128)(2,1)}, u32[]{:S(2)}, u32[]{:S(2)}) %collective-permute-start.7) | collective-permute-done | bytes 589856 | tf_op jit(solution)/shard_map/ppermute | solution.py:14
  217.1 21.0 %collective-permute-start.12 = (bf16[384,3,256]{2,0,1:T(8,128)(2,1)}, bf16[384,3,256]{2,0,1:T(8,128)(2,1)}, u32[]{:S(2)}, u32[]{:S(2)}) collective-permute-start(bf16[384,3,256]{2,0,1:T(8,128)(2,1)} %slice.214), channel_id=1, source_target_pairs={{0,8},{8,16},{16,24},{24,32},{32,40},{40,48},{48,56},{56,64},{64,7... | collective-permute-start | bytes 1769480 | tf_op jit(solution)/shard_map/ppermute | solution.py:14
  238.1 12.1 %collective-permute-start.13 = (bf16[384,3,256]{2,0,1:T(8,128)(2,1)}, bf16[384,3,256]{2,0,1:T(8,128)(2,1)}, u32[]{:S(2)}, u32[]{:S(2)}) collective-permute-start(bf16[384,3,256]{2,0,1:T(8,128)(2,1)} %slice.214), channel_id=1, source_target_pairs={{0,16},{8,24},{16,32},{24,40},{32,48},{40,56},{48,64},{56,72},{64,... | collective-permute-start | bytes 1769480 | tf_op jit(solution)/shard_map/ppermute | solution.py:14
  250.2 21.8 %collective-permute-done.9 = bf16[384,3,256]{2,0,1:T(8,128)(2,1)} collective-permute-done((bf16[384,3,256]{2,0,1:T(8,128)(2,1)}, bf16[384,3,256]{2,0,1:T(8,128)(2,1)}, u32[]{:S(2)}, u32[]{:S(2)}) %collective-permute-start.9) | collective-permute-done | bytes 589856 | tf_op jit(solution)/shard_map/ppermute | solution.py:14
  272.0 27.5 %collective-permute-start.14 = (bf16[384,3,256]{2,0,1:T(8,128)(2,1)}, bf16[384,3,256]{2,0,1:T(8,128)(2,1)}, u32[]{:S(2)}, u32[]{:S(2)}) collective-permute-start(bf16[384,3,256]{2,0,1:T(8,128)(2,1)} %slice.214), channel_id=1, source_target_pairs={{0,24},{8,32},{16,40},{24,48},{32,56},{40,64},{48,72},{56,80},{64,... | collective-permute-start | bytes 1769480 | tf_op jit(solution)/shard_map/ppermute | solution.py:14
  299.5 64.9 %collective-permute-start.15 = (bf16[384,3,256]{2,0,1:T(8,128)(2,1)}, bf16[384,3,256]{2,0,1:T(8,128)(2,1)}, u32[]{:S(2)}, u32[]{:S(2)}) collective-permute-start(bf16[384,3,256]{2,0,1:T(8,128)(2,1)} %slice.214), channel_id=1, source_target_pairs={{0,32},{8,40},{16,48},{24,56},{32,64},{40,72},{48,80},{56,88},{64,... | collective-permute-start | bytes 1769480 | tf_op jit(solution)/shard_map/ppermute | solution.py:14
  364.4 11.6 %collective-permute-start.16 = (bf16[384,3,256]{2,0,1:T(8,128)(2,1)}, bf16[384,3,256]{2,0,1:T(8,128)(2,1)}, u32[]{:S(2)}, u32[]{:S(2)}) collective-permute-start(bf16[384,3,256]{2,0,1:T(8,128)(2,1)} %slice.214), channel_id=1, source_target_pairs={{0,40},{8,48},{16,56},{24,64},{32,72},{40,80},{48,88},{56,96},{64,... | collective-permute-start | bytes 1769480 | tf_op jit(solution)/shard_map/ppermute | solution.py:14
  376.0 1.9 collective-permute-start.17
  378.0 1.9 collective-permute-start.18
  379.9 1.9 collective-permute-start.19
  381.9 7.5 %collective-permute-done.15 = bf16[384,3,256]{2,0,1:T(8,128)(2,1)} collective-permute-done((bf16[384,3,256]{2,0,1:T(8,128)(2,1)}, bf16[384,3,256]{2,0,1:T(8,128)(2,1)}, u32[]{:S(2)}, u32[]{:S(2)}) %collective-permute-start.15) | collective-permute-done | bytes 589856 | tf_op jit(solution)/shard_map/ppermute | solution.py:14
  389.3 1.9 collective-permute-start.20
  391.2 26.1 %collective-permute-done.16 = bf16[384,3,256]{2,0,1:T(8,128)(2,1)} collective-permute-done((bf16[384,3,256]{2,0,1:T(8,128)(2,1)}, bf16[384,3,256]{2,0,1:T(8,128)(2,1)}, u32[]{:S(2)}, u32[]{:S(2)}) %collective-permute-start.16) | collective-permute-done | bytes 589856 | tf_op jit(solution)/shard_map/ppermute | solution.py:14
  417.3 13.9 %collective-permute-start.21 = (bf16[384,3,256]{2,0,1:T(8,128)(2,1)}, bf16[384,3,256]{2,0,1:T(8,128)(2,1)}, u32[]{:S(2)}, u32[]{:S(2)}) collective-permute-start(bf16[384,3,256]{2,0,1:T(8,128)(2,1)} %slice.214), channel_id=1, source_target_pairs={{0,80},{8,88},{16,96},{24,104},{32,112},{40,120},{48,128},{56,136}... | collective-permute-start | bytes 1769480 | tf_op jit(solution)/shard_map/ppermute | solution.py:14
  431.3 12.6 %collective-permute-done.17 = bf16[384,3,256]{2,0,1:T(8,128)(2,1)} collective-permute-done((bf16[384,3,256]{2,0,1:T(8,128)(2,1)}, bf16[384,3,256]{2,0,1:T(8,128)(2,1)}, u32[]{:S(2)}, u32[]{:S(2)}) %collective-permute-start.17) | collective-permute-done | bytes 589856 | tf_op jit(solution)/shard_map/ppermute | solution.py:14
  443.8 1.9 collective-permute-start.22
  445.8 30.3 %collective-permute-done.18 = bf16[384,3,256]{2,0,1:T(8,128)(2,1)} collective-permute-done((bf16[384,3,256]{2,0,1:T(8,128)(2,1)}, bf16[384,3,256]{2,0,1:T(8,128)(2,1)}, u32[]{:S(2)}, u32[]{:S(2)}) %collective-permute-start.18) | collective-permute-done | bytes 589856 | tf_op jit(solution)/shard_map/ppermute | solution.py:14
  476.1 1.9 collective-permute-start.23
  573.9 5.5 conditional.25
  573.9 1.4 fusion
  577.7 1.7 convolution_add_fusion
  579.7 8.1 %conditional.34 = ((f32[3,384]{1,0:T(4,128)}, f32[3,384]{1,0:T(4,128)S(1)}, f32[3,384,128]{2,1,0:T(8,128)S(1)})) conditional(s32[]{:T(128)} %bitcast.106, (f32[3,384]{1,0:T(4,128)}, f32[3,384]{1,0:T(4,128)S(1)}, f32[3,384,128]{2,1,0:T(8,128)S(1)}) %get-tuple-element.1021, (pred[1]{0:T(512)(128)(4,1)}, bf16[384,3,256]{2,0,1:T(8,128)(2,1)}, ...), branch_computations={%region_38.39_spmd, %region_39.42_spmd} | conditional | flops 232540416 | bytes 7447585 | solution.py:80
  587.8 5.6 conditional.35
  591.6 1.8 convolution_add_fusion.10
  593.4 6.3 conditional.37
  598.0 1.8 convolution_add_fusion.12
  599.8 5.6 conditional.39
  599.8 1.4 fusion.211
  603.6 1.8 convolution_add_fusion.14
  605.4 5.6 conditional.40
  605.4 1.4 fusion.226
  609.2 1.8 convolution_add_fusion.15
  611.0 6.0 conditional.41
  615.2 1.8 convolution_add_fusion.16
  617.0 5.6 conditional.43
  617.1 1.4 fusion.271
  620.9 1.8 convolution_add_fusion.18
  622.7 5.6 conditional.44
  622.7 1.4 fusion.286
  626.5 1.8 convolution_add_fusion.19
  628.3 5.6 conditional.45
  632.1 1.8 convolution_add_fusion.20
  634.5 2.8 convolution_convert_fusion
  637.4 39.5 %reduce-scatter.2.cloned.1.call-done = bf16[48,3072]{1,0:T(8,128)(2,1)} async-done(((bf16[384,3072]{1,0:T(8,128)(2,1)}), bf16[48,3072]{1,0:T(8,128)(2,1)}) %reduce-scatter.2.cloned.1.call-update) | async-done | bytes 294928 | tf_op jit(solution)/shard_map/reduce_scatter | solution.py:101
  676.8 1.7 multiply_convert_fusion
  (94 shorter events, 37.3 us)
Async XLA Ops:
  6.5 627.9 %copy-start = (bf16[384,3072]{1,0:T(8,128)(2,1)S(1)}, bf16[384,3072]{1,0:T(8,128)(2,1)}, u32[]{:S(2)}) copy-start(bf16[384,3072]{1,0:T(8,128)(2,1)} %param.63) | copy-start | bytes 7077892
  6.5 36.4 %all-gather.2.cloned.1.call-start = ((), (), s32[]{:S(2)}) async-start(), calls=%async_computation.1 | async-start | bytes 2654208 | tf_op jit(solution)/shard_map/all_gather | solution.py:29
  11.6 466.4 %copy-start.2 = (s32[32]{0:T(128)S(1)}, s32[32]{0:T(128)}, u32[]{:S(2)}) copy-start(s32[32]{0:T(128)} %param.64) | copy-start | bytes 388
  11.6 469.6 %copy-start.4 = (s32[32,2]{0,1:T(2,128)S(1)}, s32[32,2]{0,1:T(2,128)}, u32[]{:S(2)}) copy-start(s32[32,2]{0,1:T(2,128)} %param.65) | copy-start | bytes 772
  11.6 665.2 %reduce-scatter.2.cloned.1.call-start = ((), (), s32[]{:S(2)}) async-start(), calls=%async_computation.2 | async-start | bytes 2654208 | tf_op jit(solution)/shard_map/reduce_scatter | solution.py:101
  49.8 0.9 copy-start.1
  51.6 33.7 %collective-permute-start = (bf16[384,3,256]{2,0,1:T(8,128)(2,1)}, bf16[384,3,256]{2,0,1:T(8,128)(2,1)}, u32[]{:S(2)}, u32[]{:S(2)}) collective-permute-start(bf16[384,3,256]{2,0,1:T(8,128)(2,1)} %slice.214), channel_id=1, source_target_pairs={{96,0},{104,8},{112,16},{120,24},{128,32},{136,40},{144,48},{152,5... | collective-permute-start | bytes 1769480 | tf_op jit(solution)/shard_map/ppermute | solution.py:14
  59.2 66.8 %collective-permute-start.1 = (bf16[384,3,256]{2,0,1:T(8,128)(2,1)}, bf16[384,3,256]{2,0,1:T(8,128)(2,1)}, u32[]{:S(2)}, u32[]{:S(2)}) collective-permute-start(bf16[384,3,256]{2,0,1:T(8,128)(2,1)} %slice.214), channel_id=1, source_target_pairs={{88,0},{96,8},{104,16},{112,24},{120,32},{128,40},{136,48},{144,56... | collective-permute-start | bytes 1769480 | tf_op jit(solution)/shard_map/ppermute | solution.py:14
  61.2 90.0 %collective-permute-start.2 = (bf16[384,3,256]{2,0,1:T(8,128)(2,1)}, bf16[384,3,256]{2,0,1:T(8,128)(2,1)}, u32[]{:S(2)}, u32[]{:S(2)}) collective-permute-start(bf16[384,3,256]{2,0,1:T(8,128)(2,1)} %slice.214), channel_id=1, source_target_pairs={{80,0},{88,8},{96,16},{104,24},{112,32},{120,40},{128,48},{136,56}... | collective-permute-start | bytes 1769480 | tf_op jit(solution)/shard_map/ppermute | solution.py:14
  63.1 102.3 %collective-permute-start.3 = (bf16[384,3,256]{2,0,1:T(8,128)(2,1)}, bf16[384,3,256]{2,0,1:T(8,128)(2,1)}, u32[]{:S(2)}, u32[]{:S(2)}) collective-permute-start(bf16[384,3,256]{2,0,1:T(8,128)(2,1)} %slice.214), channel_id=1, source_target_pairs={{72,0},{80,8},{88,16},{96,24},{104,32},{112,40},{120,48},{128,56},... | collective-permute-start | bytes 1769480 | tf_op jit(solution)/shard_map/ppermute | solution.py:14
  65.0 107.4 %collective-permute-start.4 = (bf16[384,3,256]{2,0,1:T(8,128)(2,1)}, bf16[384,3,256]{2,0,1:T(8,128)(2,1)}, u32[]{:S(2)}, u32[]{:S(2)}) collective-permute-start(bf16[384,3,256]{2,0,1:T(8,128)(2,1)} %slice.214), channel_id=1, source_target_pairs={{64,0},{72,8},{80,16},{88,24},{96,32},{104,40},{112,48},{120,56},{... | collective-permute-start | bytes 1769480 | tf_op jit(solution)/shard_map/ppermute | solution.py:14
  85.3 104.2 %collective-permute-start.5 = (bf16[384,3,256]{2,0,1:T(8,128)(2,1)}, bf16[384,3,256]{2,0,1:T(8,128)(2,1)}, u32[]{:S(2)}, u32[]{:S(2)}) collective-permute-start(bf16[384,3,256]{2,0,1:T(8,128)(2,1)} %slice.214), channel_id=1, source_target_pairs={{56,0},{64,8},{72,16},{80,24},{88,32},{96,40},{104,48},{112,56},{1... | collective-permute-start | bytes 1769480 | tf_op jit(solution)/shard_map/ppermute | solution.py:14
  126.0 65.4 %collective-permute-start.6 = (bf16[384,3,256]{2,0,1:T(8,128)(2,1)}, bf16[384,3,256]{2,0,1:T(8,128)(2,1)}, u32[]{:S(2)}, u32[]{:S(2)}) collective-permute-start(bf16[384,3,256]{2,0,1:T(8,128)(2,1)} %slice.214), channel_id=1, source_target_pairs={{48,0},{56,8},{64,16},{72,24},{80,32},{88,40},{96,48},{104,56},{11... | collective-permute-start | bytes 1769480 | tf_op jit(solution)/shard_map/ppermute | solution.py:14
  151.1 66.0 %collective-permute-start.7 = (bf16[384,3,256]{2,0,1:T(8,128)(2,1)}, bf16[384,3,256]{2,0,1:T(8,128)(2,1)}, u32[]{:S(2)}, u32[]{:S(2)}) collective-permute-start(bf16[384,3,256]{2,0,1:T(8,128)(2,1)} %slice.214), channel_id=1, source_target_pairs={{40,0},{48,8},{56,16},{64,24},{72,32},{80,40},{88,48},{96,56},{104... | collective-permute-start | bytes 1769480 | tf_op jit(solution)/shard_map/ppermute | solution.py:14
  165.4 72.7 %collective-permute-start.8 = (bf16[384,3,256]{2,0,1:T(8,128)(2,1)}, bf16[384,3,256]{2,0,1:T(8,128)(2,1)}, u32[]{:S(2)}, u32[]{:S(2)}) collective-permute-start(bf16[384,3,256]{2,0,1:T(8,128)(2,1)} %slice.214), channel_id=1, source_target_pairs={{32,0},{40,8},{48,16},{56,24},{64,32},{72,40},{80,48},{88,56},{96,... | collective-permute-start | bytes 1769480 | tf_op jit(solution)/shard_map/ppermute | solution.py:14
  172.4 99.6 %collective-permute-start.9 = (bf16[384,3,256]{2,0,1:T(8,128)(2,1)}, bf16[384,3,256]{2,0,1:T(8,128)(2,1)}, u32[]{:S(2)}, u32[]{:S(2)}) collective-permute-start(bf16[384,3,256]{2,0,1:T(8,128)(2,1)} %slice.214), channel_id=1, source_target_pairs={{24,0},{32,8},{40,16},{48,24},{56,32},{64,40},{72,48},{80,56},{88,... | collective-permute-start | bytes 1769480 | tf_op jit(solution)/shard_map/ppermute | solution.py:14
  189.4 110.1 %collective-permute-start.10 = (bf16[384,3,256]{2,0,1:T(8,128)(2,1)}, bf16[384,3,256]{2,0,1:T(8,128)(2,1)}, u32[]{:S(2)}, u32[]{:S(2)}) collective-permute-start(bf16[384,3,256]{2,0,1:T(8,128)(2,1)} %slice.214), channel_id=1, source_target_pairs={{16,0},{24,8},{32,16},{40,24},{48,32},{56,40},{64,48},{72,56},{80,... | collective-permute-start | bytes 1769480 | tf_op jit(solution)/shard_map/ppermute | solution.py:14
  191.4 173.0 %collective-permute-start.11 = (bf16[384,3,256]{2,0,1:T(8,128)(2,1)}, bf16[384,3,256]{2,0,1:T(8,128)(2,1)}, u32[]{:S(2)}, u32[]{:S(2)}) collective-permute-start(bf16[384,3,256]{2,0,1:T(8,128)(2,1)} %slice.214), channel_id=1, source_target_pairs={{8,0},{16,8},{24,16},{32,24},{40,32},{48,40},{56,48},{64,56},{72,6... | collective-permute-start | bytes 1769480 | tf_op jit(solution)/shard_map/ppermute | solution.py:14
  217.1 158.9 %collective-permute-start.12 = (bf16[384,3,256]{2,0,1:T(8,128)(2,1)}, bf16[384,3,256]{2,0,1:T(8,128)(2,1)}, u32[]{:S(2)}, u32[]{:S(2)}) collective-permute-start(bf16[384,3,256]{2,0,1:T(8,128)(2,1)} %slice.214), channel_id=1, source_target_pairs={{0,8},{8,16},{16,24},{24,32},{32,40},{40,48},{48,56},{56,64},{64,7... | collective-permute-start | bytes 1769480 | tf_op jit(solution)/shard_map/ppermute | solution.py:14
  238.1 139.8 %collective-permute-start.13 = (bf16[384,3,256]{2,0,1:T(8,128)(2,1)}, bf16[384,3,256]{2,0,1:T(8,128)(2,1)}, u32[]{:S(2)}, u32[]{:S(2)}) collective-permute-start(bf16[384,3,256]{2,0,1:T(8,128)(2,1)} %slice.214), channel_id=1, source_target_pairs={{0,16},{8,24},{16,32},{24,40},{32,48},{40,56},{48,64},{56,72},{64,... | collective-permute-start | bytes 1769480 | tf_op jit(solution)/shard_map/ppermute | solution.py:14
  272.0 107.9 %collective-permute-start.14 = (bf16[384,3,256]{2,0,1:T(8,128)(2,1)}, bf16[384,3,256]{2,0,1:T(8,128)(2,1)}, u32[]{:S(2)}, u32[]{:S(2)}) collective-permute-start(bf16[384,3,256]{2,0,1:T(8,128)(2,1)} %slice.214), channel_id=1, source_target_pairs={{0,24},{8,32},{16,40},{24,48},{32,56},{40,64},{48,72},{56,80},{64,... | collective-permute-start | bytes 1769480 | tf_op jit(solution)/shard_map/ppermute | solution.py:14
  299.5 89.8 %collective-permute-start.15 = (bf16[384,3,256]{2,0,1:T(8,128)(2,1)}, bf16[384,3,256]{2,0,1:T(8,128)(2,1)}, u32[]{:S(2)}, u32[]{:S(2)}) collective-permute-start(bf16[384,3,256]{2,0,1:T(8,128)(2,1)} %slice.214), channel_id=1, source_target_pairs={{0,32},{8,40},{16,48},{24,56},{32,64},{40,72},{48,80},{56,88},{64,... | collective-permute-start | bytes 1769480 | tf_op jit(solution)/shard_map/ppermute | solution.py:14
  364.4 52.9 %collective-permute-start.16 = (bf16[384,3,256]{2,0,1:T(8,128)(2,1)}, bf16[384,3,256]{2,0,1:T(8,128)(2,1)}, u32[]{:S(2)}, u32[]{:S(2)}) collective-permute-start(bf16[384,3,256]{2,0,1:T(8,128)(2,1)} %slice.214), channel_id=1, source_target_pairs={{0,40},{8,48},{16,56},{24,64},{32,72},{40,80},{48,88},{56,96},{64,... | collective-permute-start | bytes 1769480 | tf_op jit(solution)/shard_map/ppermute | solution.py:14
  376.0 67.8 %collective-permute-start.17 = (bf16[384,3,256]{2,0,1:T(8,128)(2,1)}, bf16[384,3,256]{2,0,1:T(8,128)(2,1)}, u32[]{:S(2)}, u32[]{:S(2)}) collective-permute-start(bf16[384,3,256]{2,0,1:T(8,128)(2,1)} %slice.214), channel_id=1, source_target_pairs={{0,48},{8,56},{16,64},{24,72},{32,80},{40,88},{48,96},{56,104},{64... | collective-permute-start | bytes 1769480 | tf_op jit(solution)/shard_map/ppermute | solution.py:14
  378.0 98.1 %collective-permute-start.18 = (bf16[384,3,256]{2,0,1:T(8,128)(2,1)}, bf16[384,3,256]{2,0,1:T(8,128)(2,1)}, u32[]{:S(2)}, u32[]{:S(2)}) collective-permute-start(bf16[384,3,256]{2,0,1:T(8,128)(2,1)} %slice.214), channel_id=1, source_target_pairs={{0,56},{8,64},{16,72},{24,80},{32,88},{40,96},{48,104},{56,112},{6... | collective-permute-start | bytes 1769480 | tf_op jit(solution)/shard_map/ppermute | solution.py:14
  379.9 248.4 %collective-permute-start.19 = (bf16[384,3,256]{2,0,1:T(8,128)(2,1)}, bf16[384,3,256]{2,0,1:T(8,128)(2,1)}, u32[]{:S(2)}, u32[]{:S(2)}) collective-permute-start(bf16[384,3,256]{2,0,1:T(8,128)(2,1)} %slice.214), channel_id=1, source_target_pairs={{0,64},{8,72},{16,80},{24,88},{32,96},{40,104},{48,112},{56,120},{... | collective-permute-start | bytes 1769480 | tf_op jit(solution)/shard_map/ppermute | solution.py:14
  389.3 244.6 %collective-permute-start.20 = (bf16[384,3,256]{2,0,1:T(8,128)(2,1)}, bf16[384,3,256]{2,0,1:T(8,128)(2,1)}, u32[]{:S(2)}, u32[]{:S(2)}) collective-permute-start(bf16[384,3,256]{2,0,1:T(8,128)(2,1)} %slice.214), channel_id=1, source_target_pairs={{0,72},{8,80},{16,88},{24,96},{32,104},{40,112},{48,120},{56,128},... | collective-permute-start | bytes 1769480 | tf_op jit(solution)/shard_map/ppermute | solution.py:14
  417.3 216.6 %collective-permute-start.21 = (bf16[384,3,256]{2,0,1:T(8,128)(2,1)}, bf16[384,3,256]{2,0,1:T(8,128)(2,1)}, u32[]{:S(2)}, u32[]{:S(2)}) collective-permute-start(bf16[384,3,256]{2,0,1:T(8,128)(2,1)} %slice.214), channel_id=1, source_target_pairs={{0,80},{8,88},{16,96},{24,104},{32,112},{40,120},{48,128},{56,136}... | collective-permute-start | bytes 1769480 | tf_op jit(solution)/shard_map/ppermute | solution.py:14
  443.8 190.1 %collective-permute-start.22 = (bf16[384,3,256]{2,0,1:T(8,128)(2,1)}, bf16[384,3,256]{2,0,1:T(8,128)(2,1)}, u32[]{:S(2)}, u32[]{:S(2)}) collective-permute-start(bf16[384,3,256]{2,0,1:T(8,128)(2,1)} %slice.214), channel_id=1, source_target_pairs={{0,88},{8,96},{16,104},{24,112},{32,120},{40,128},{48,136},{56,144... | collective-permute-start | bytes 1769480 | tf_op jit(solution)/shard_map/ppermute | solution.py:14
  476.1 158.1 %collective-permute-start.23 = (bf16[384,3,256]{2,0,1:T(8,128)(2,1)}, bf16[384,3,256]{2,0,1:T(8,128)(2,1)}, u32[]{:S(2)}, u32[]{:S(2)}) collective-permute-start(bf16[384,3,256]{2,0,1:T(8,128)(2,1)} %slice.214), channel_id=1, source_target_pairs={{0,96},{8,104},{16,112},{24,120},{32,128},{40,136},{48,144},{56,15... | collective-permute-start | bytes 1769480 | tf_op jit(solution)/shard_map/ppermute | solution.py:14
  637.3 39.5 %copy-start.3 = (f32[3072]{0:T(1024)S(1)}, f32[3072]{0:T(1024)}, u32[]{:S(2)}) copy-start(f32[3072]{0:T(1024)} %param.61) | copy-start | bytes 36868
Sparse Core Ops, SparseCore 0:
  11.7 31.0 all-gather.1
  637.5 39.3 reduce-scatter.1
where the time goes:
time: 697 us; the launch traced here: 686 us
  waiting for transfers between devices  281 us (40%)
  starting transfers between devices  216 us (31%)
  between operations  107 us (15%)
  matrix products  38.1 us (5%)
  other arithmetic  25.2 us (4%)
  local copies, waits for them, and re-layouts  9.26 us (1%)
  loops' own time  9.18 us (1%)
    ppermute x24, starting transfers between devices, from_behind(): return lax.ppermute(block, axis, route)  216 us
    ppermute x24, waiting for transfers between devices, from_behind(): return lax.ppermute(block, axis, route)  210 us
    reduce_scatter x1, waiting for transfers between devices, on_device(): lax.psum_scatter(jnp.dot(attn, w_out, preferred_element_type=jnp.float32)...  39.5 us
    all_gather x1, waiting for transfers between devices, on_device(): lax.all_gather(normed, 'uly', axis=0, tiled=True)  31.2 us
    dot_general x9, matrix products, compute(): jnp.einsum('hqk,khd->hqd', weights, kv_tile[:, :, head_dim:], preferred_e...  15.8 us
  transfers between devices with their start and end apart: 26, of which 12 were waited for; matrix products, arithmetic and copies ran while one was open for 8% of the time, Pallas kernels for 0%

commit v1 on v0

--- a/solution.py
+++ b/solution.py
@@ -15,6 +15,18 @@
 
 
 def on_device(tokens, mod_shift, mod_scale, out_gate, w_qkv, w_out, tile_map, window_corner):
+
+    def push_threads(group_axis, array_axis, sample):
+        width = lax.axis_size(group_axis)
+        e_now = lax.all_to_all(
+            jnp.tile(sample, [width if d == array_axis else 1 for d in range(sample.ndim)]),
+            axis_name=group_axis,
+            split_axis=array_axis,
+            concat_axis=array_axis,
+            tiled=True,
+        )
+        return e_now
+
     values_in = tokens.astype(jnp.float32)
     mean_row = jnp.mean(values_in, axis=-1, keepdims=True)
     centred = values_in - mean_row
@@ -26,7 +38,7 @@
     head_dim = w_qkv.shape[2] // 3
     qkv = jnp.einsum(
         "td,dhe->the",
-        lax.all_gather(normed, "uly", axis=0, tiled=True),
+        push_threads("uly", array_axis=0, sample=normed),
         w_qkv,
         preferred_element_type=jnp.float32,
     ).astype(jnp.bfloat16)

time: 697 us -> 670 us (0.961)
  starting transfers between devices: 216 us -> 168 us
  blocking collectives: 0 us -> 34.9 us
  waiting for transfers between devices: 281 us -> 273 us
    ppermute x24, starting transfers between devices: 216 us -> 168 us  [from_behind(): return lax.ppermute(block, axis, route)]
    all_to_all x0 -> x1, blocking collectives: none -> 34.9 us  [push_threads(): lax.all_to_all(jnp.tile(sample, [width if d == array_axis else 1 for d in...]
    all_gather x1 -> x0, waiting for transfers between devices: 31.2 us -> none  [on_device(): lax.all_gather(normed, 'uly', axis=0, tiled=True)]
    reduce_scatter x1, waiting for transfers between devices: 39.5 us -> 59.5 us  [on_device(): lax.psum_scatter(jnp.dot(attn, w_out, preferred_element_type=jnp.float32)...]
  transfers between devices with their start and end apart: 26 -> 25, of which waited for: 12 -> 11; matrix products, arithmetic and copies ran while one was open for 8% -> 8% of each run, Pallas kernels for 0% -> 0%
where the time goes in v1:
time: 670 us; the launch traced here: 659 us
  waiting for transfers between devices  273 us (41%)
  starting transfers between devices  168 us (25%)
  between operations  106 us (16%)
  blocking collectives  34.9 us (5%)
  matrix products  34.4 us (5%)
  other arithmetic  24.5 us (4%)
  local copies, waits for them, and re-layouts  9.49 us (1%)
  loops' own time  9.06 us (1%)
    ppermute x24, waiting for transfers between devices, from_behind(): return lax.ppermute(block, axis, route)  213 us
    ppermute x24, starting transfers between devices, from_behind(): return lax.ppermute(block, axis, route)  168 us
    reduce_scatter x1, waiting for transfers between devices, on_device(): lax.psum_scatter(jnp.dot(attn, w_out, preferred_element_type=jnp.float32)...  59.5 us
    all_to_all x1, blocking collectives, push_threads(): lax.all_to_all(jnp.tile(sample, [width if d == array_axis else 1 for d in...  34.9 us
    dot_general x9, matrix products, compute(): jnp.einsum('hqk,khd->hqd', weights, kv_tile[:, :, head_dim:], preferred_e...  15.8 us
  transfers between devices with their start and end apart: 25, of which 11 were waited for; matrix products, arithmetic and copies ran while one was open for 8% of the time, Pallas kernels for 0%

profile of v1, /device:TPU:4, one launch (start us, length us, event | category | flops | bytes accessed | tf_op | source)
XLA Modules:
  0.0 659.0 jit_solution(14448534223743909291)
XLA Ops:
  11.2 34.9 %all_to_all.9 = bf16[8,48,3072]{2,1,0:T(8,128)(2,1)S(1)} all-to-all(bf16[8,48,3072]{2,1,0:T(8,128)(2,1)S(1)} %tile.2), channel_id=1, replica_groups=mesh['blk'=32,'uly'=8] {'uly'}, dimensions={0} | all-to-all | bytes 4718592 | tf_op jit(solution)/shard_map/all_to_all | solution.py:21
  46.1 3.2 convolution_convert_fusion.1
  51.1 9.0 %collective-permute-start = (bf16[384,3,256]{2,0,1:T(8,128)(2,1)}, bf16[384,3,256]{2,0,1:T(8,128)(2,1)}, u32[]{:S(2)}, u32[]{:S(2)}) collective-permute-start(bf16[384,3,256]{2,0,1:T(8,128)(2,1)} %slice.214), channel_id=1, source_target_pairs={{96,0},{104,8},{112,16},{120,24},{128,32},{136,40},{144,48},{152,5... | collective-permute-start | bytes 1769480 | tf_op jit(solution)/shard_map/ppermute | solution.py:14
  60.2 1.9 collective-permute-start.1
  62.1 1.9 collective-permute-start.2
  64.0 1.9 collective-permute-start.3
  65.9 1.9 collective-permute-start.4
  67.9 17.7 %collective-permute-done = bf16[384,3,256]{2,0,1:T(8,128)(2,1)} collective-permute-done((bf16[384,3,256]{2,0,1:T(8,128)(2,1)}, bf16[384,3,256]{2,0,1:T(8,128)(2,1)}, u32[]{:S(2)}, u32[]{:S(2)}) %collective-permute-start) | collective-permute-done | bytes 589856 | tf_op jit(solution)/shard_map/ppermute | solution.py:14
  85.6 7.6 %collective-permute-start.5 = (bf16[384,3,256]{2,0,1:T(8,128)(2,1)}, bf16[384,3,256]{2,0,1:T(8,128)(2,1)}, u32[]{:S(2)}, u32[]{:S(2)}) collective-permute-start(bf16[384,3,256]{2,0,1:T(8,128)(2,1)} %slice.214), channel_id=1, source_target_pairs={{56,0},{64,8},{72,16},{80,24},{88,32},{96,40},{104,48},{112,56},{1... | collective-permute-start | bytes 1769480 | tf_op jit(solution)/shard_map/ppermute | solution.py:14
  93.2 33.0 %collective-permute-done.1 = bf16[384,3,256]{2,0,1:T(8,128)(2,1)} collective-permute-done((bf16[384,3,256]{2,0,1:T(8,128)(2,1)}, bf16[384,3,256]{2,0,1:T(8,128)(2,1)}, u32[]{:S(2)}, u32[]{:S(2)}) %collective-permute-start.1) | collective-permute-done | bytes 589856 | tf_op jit(solution)/shard_map/ppermute | solution.py:14
  126.1 1.9 collective-permute-start.6
  128.1 21.5 %collective-permute-done.2 = bf16[384,3,256]{2,0,1:T(8,128)(2,1)} collective-permute-done((bf16[384,3,256]{2,0,1:T(8,128)(2,1)}, bf16[384,3,256]{2,0,1:T(8,128)(2,1)}, u32[]{:S(2)}, u32[]{:S(2)}) %collective-permute-start.2) | collective-permute-done | bytes 589856 | tf_op jit(solution)/shard_map/ppermute | solution.py:14
  149.6 1.9 collective-permute-start.7
  151.5 13.0 %collective-permute-done.3 = bf16[384,3,256]{2,0,1:T(8,128)(2,1)} collective-permute-done((bf16[384,3,256]{2,0,1:T(8,128)(2,1)}, bf16[384,3,256]{2,0,1:T(8,128)(2,1)}, u32[]{:S(2)}, u32[]{:S(2)}) %collective-permute-start.3) | collective-permute-done | bytes 589856 | tf_op jit(solution)/shard_map/ppermute | solution.py:14
  164.5 5.3 collective-permute-start.8
  169.8 44.7 %collective-permute-start.9 = (bf16[384,3,256]{2,0,1:T(8,128)(2,1)}, bf16[384,3,256]{2,0,1:T(8,128)(2,1)}, u32[]{:S(2)}, u32[]{:S(2)}) collective-permute-start(bf16[384,3,256]{2,0,1:T(8,128)(2,1)} %slice.214), channel_id=1, source_target_pairs={{24,0},{32,8},{40,16},{48,24},{56,32},{64,40},{72,48},{80,56},{88,... | collective-permute-start | bytes 1769480 | tf_op jit(solution)/shard_map/ppermute | solution.py:14
  214.5 1.9 collective-permute-start.10
  216.5 2.5 collective-permute-start.11
  219.0 8.9 %collective-permute-start.12 = (bf16[384,3,256]{2,0,1:T(8,128)(2,1)}, bf16[384,3,256]{2,0,1:T(8,128)(2,1)}, u32[]{:S(2)}, u32[]{:S(2)}) collective-permute-start(bf16[384,3,256]{2,0,1:T(8,128)(2,1)} %slice.214), channel_id=1, source_target_pairs={{0,8},{8,16},{16,24},{24,32},{32,40},{40,48},{48,56},{56,64},{64,7... | collective-permute-start | bytes 1769480 | tf_op jit(solution)/shard_map/ppermute | solution.py:14
  227.9 5.8 collective-permute-done.8
  233.6 9.2 %collective-permute-start.13 = (bf16[384,3,256]{2,0,1:T(8,128)(2,1)}, bf16[384,3,256]{2,0,1:T(8,128)(2,1)}, u32[]{:S(2)}, u32[]{:S(2)}) collective-permute-start(bf16[384,3,256]{2,0,1:T(8,128)(2,1)} %slice.214), channel_id=1, source_target_pairs={{0,16},{8,24},{16,32},{24,40},{32,48},{40,56},{48,64},{56,72},{64,... | collective-permute-start | bytes 1769480 | tf_op jit(solution)/shard_map/ppermute | solution.py:14
  242.8 13.9 %collective-permute-done.9 = bf16[384,3,256]{2,0,1:T(8,128)(2,1)} collective-permute-done((bf16[384,3,256]{2,0,1:T(8,128)(2,1)}, bf16[384,3,256]{2,0,1:T(8,128)(2,1)}, u32[]{:S(2)}, u32[]{:S(2)}) %collective-permute-start.9) | collective-permute-done | bytes 589856 | tf_op jit(solution)/shard_map/ppermute | solution.py:14
  256.8 8.5 %collective-permute-start.14 = (bf16[384,3,256]{2,0,1:T(8,128)(2,1)}, bf16[384,3,256]{2,0,1:T(8,128)(2,1)}, u32[]{:S(2)}, u32[]{:S(2)}) collective-permute-start(bf16[384,3,256]{2,0,1:T(8,128)(2,1)} %slice.214), channel_id=1, source_target_pairs={{0,24},{8,32},{16,40},{24,48},{32,56},{40,64},{48,72},{56,80},{64,... | collective-permute-start | bytes 1769480 | tf_op jit(solution)/shard_map/ppermute | solution.py:14
  265.3 19.2 %collective-permute-done.10 = bf16[384,3,256]{2,0,1:T(8,128)(2,1)} collective-permute-done((bf16[384,3,256]{2,0,1:T(8,128)(2,1)}, bf16[384,3,256]{2,0,1:T(8,128)(2,1)}, u32[]{:S(2)}, u32[]{:S(2)}) %collective-permute-start.10) | collective-permute-done | bytes 589856 | tf_op jit(solution)/shard_map/ppermute | solution.py:14
  284.5 4.6 collective-permute-start.15
  289.1 39.6 %collective-permute-done.11 = bf16[384,3,256]{2,0,1:T(8,128)(2,1)} collective-permute-done((bf16[384,3,256]{2,0,1:T(8,128)(2,1)}, bf16[384,3,256]{2,0,1:T(8,128)(2,1)}, u32[]{:S(2)}, u32[]{:S(2)}) %collective-permute-start.11) | collective-permute-done | bytes 589856 | tf_op jit(solution)/shard_map/ppermute | solution.py:14
  328.6 1.9 collective-permute-start.16
  330.6 30.7 %collective-permute-start.17 = (bf16[384,3,256]{2,0,1:T(8,128)(2,1)}, bf16[384,3,256]{2,0,1:T(8,128)(2,1)}, u32[]{:S(2)}, u32[]{:S(2)}) collective-permute-start(bf16[384,3,256]{2,0,1:T(8,128)(2,1)} %slice.214), channel_id=1, source_target_pairs={{0,48},{8,56},{16,64},{24,72},{32,80},{40,88},{48,96},{56,104},{64... | collective-permute-start | bytes 1769480 | tf_op jit(solution)/shard_map/ppermute | solution.py:14
  361.3 11.6 %collective-permute-start.18 = (bf16[384,3,256]{2,0,1:T(8,128)(2,1)}, bf16[384,3,256]{2,0,1:T(8,128)(2,1)}, u32[]{:S(2)}, u32[]{:S(2)}) collective-permute-start(bf16[384,3,256]{2,0,1:T(8,128)(2,1)} %slice.214), channel_id=1, source_target_pairs={{0,56},{8,64},{16,72},{24,80},{32,88},{40,96},{48,104},{56,112},{6... | collective-permute-start | bytes 1769480 | tf_op jit(solution)/shard_map/ppermute | solution.py:14
  373.0 1.9 collective-permute-start.19
  374.9 1.9 collective-permute-start.20
  376.9 1.9 collective-permute-start.21
  378.8 18.6 %collective-permute-done.17 = bf16[384,3,256]{2,0,1:T(8,128)(2,1)} collective-permute-done((bf16[384,3,256]{2,0,1:T(8,128)(2,1)}, bf16[384,3,256]{2,0,1:T(8,128)(2,1)}, u32[]{:S(2)}, u32[]{:S(2)}) %collective-permute-start.17) | collective-permute-done | bytes 589856 | tf_op jit(solution)/shard_map/ppermute | solution.py:14
  397.4 1.9 collective-permute-start.22
  399.4 31.0 %collective-permute-done.18 = bf16[384,3,256]{2,0,1:T(8,128)(2,1)} collective-permute-done((bf16[384,3,256]{2,0,1:T(8,128)(2,1)}, bf16[384,3,256]{2,0,1:T(8,128)(2,1)}, u32[]{:S(2)}, u32[]{:S(2)}) %collective-permute-start.18) | collective-permute-done | bytes 589856 | tf_op jit(solution)/shard_map/ppermute | solution.py:14
  430.4 1.9 collective-permute-start.23
  527.5 5.5 conditional.25
  527.5 1.4 fusion
  529.5 1.6 convolution_add_fusion
  533.3 8.1 %conditional.34 = ((f32[3,384]{1,0:T(4,128)}, f32[3,384]{1,0:T(4,128)S(1)}, f32[3,384,128]{2,1,0:T(8,128)S(1)})) conditional(s32[]{:T(128)} %bitcast.106, (f32[3,384]{1,0:T(4,128)}, f32[3,384]{1,0:T(4,128)S(1)}, f32[3,384,128]{2,1,0:T(8,128)S(1)}) %get-tuple-element.1021, (pred[1]{0:T(512)(128)(4,1)}, bf16[384,3,256]{2,0,1:T(8,128)(2,1)}, ...), branch_computations={%region_38.39_spmd, %region_39.42_spmd} | conditional | flops 232540416 | bytes 7447585 | solution.py:92
  541.4 5.6 conditional.35
  541.4 1.4 fusion.151
  544.6 1.8 convolution_add_fusion.10
  547.0 6.3 conditional.37
  547.0 1.4 fusion.181
  551.5 1.8 convolution_add_fusion.12
  553.3 5.6 conditional.39
  553.3 1.4 fusion.211
  556.6 1.8 convolution_add_fusion.14
  558.9 5.6 conditional.40
  562.2 1.8 convolution_add_fusion.15
  564.5 6.0 conditional.41
  564.9 1.4 fusion.241
  568.1 1.8 convolution_add_fusion.16
  570.5 5.6 conditional.43
  573.7 1.8 convolution_add_fusion.18
  576.1 5.6 conditional.44
  579.3 1.8 convolution_add_fusion.19
  581.7 5.6 conditional.45
  581.7 1.4 fusion.301
  584.9 1.8 convolution_add_fusion.20
  587.8 2.8 convolution_convert_fusion
  590.7 59.5 %reduce-scatter.2.cloned.1.call-done = bf16[48,3072]{1,0:T(8,128)(2,1)} async-done(((bf16[384,3072]{1,0:T(8,128)(2,1)}), bf16[48,3072]{1,0:T(8,128)(2,1)}) %reduce-scatter.2.cloned.1.call-update) | async-done | bytes 294928 | tf_op jit(solution)/shard_map/reduce_scatter | solution.py:113
  650.2 1.7 multiply_convert_fusion
  (95 shorter events, 37.1 us)
Async XLA Ops:
  6.5 581.3 %copy-start = (bf16[384,3072]{1,0:T(8,128)(2,1)S(1)}, bf16[384,3072]{1,0:T(8,128)(2,1)}, u32[]{:S(2)}) copy-start(bf16[384,3072]{1,0:T(8,128)(2,1)} %param.63) | copy-start | bytes 7077892
  6.5 643.7 %reduce-scatter.2.cloned.1.call-start = ((), (), s32[]{:S(2)}) async-start(), calls=%async_computation.2 | async-start | bytes 2654208 | tf_op jit(solution)/shard_map/reduce_scatter | solution.py:113
  10.9 35.2 %copy-start.5 = (bf16[3072,3,384]{2,0,1:T(8,128)(2,1)S(1)}, bf16[3072,3,384]{2,0,1:T(8,128)(2,1)}, u32[]{:S(2)}) copy-start(bf16[3072,3,384]{2,0,1:T(8,128)(2,1)} %param.62) | copy-start | bytes 21233668
  46.1 386.3 %copy-start.2 = (s32[32]{0:T(128)S(1)}, s32[32]{0:T(128)}, u32[]{:S(2)}) copy-start(s32[32]{0:T(128)} %param.64) | copy-start | bytes 388
  46.1 389.7 %copy-start.4 = (s32[32,2]{0,1:T(2,128)S(1)}, s32[32,2]{0,1:T(2,128)}, u32[]{:S(2)}) copy-start(s32[32,2]{0,1:T(2,128)} %param.65) | copy-start | bytes 772
  49.3 0.9 copy-start.1
  51.1 34.4 %collective-permute-start = (bf16[384,3,256]{2,0,1:T(8,128)(2,1)}, bf16[384,3,256]{2,0,1:T(8,128)(2,1)}, u32[]{:S(2)}, u32[]{:S(2)}) collective-permute-start(bf16[384,3,256]{2,0,1:T(8,128)(2,1)} %slice.214), channel_id=1, source_target_pairs={{96,0},{104,8},{112,16},{120,24},{128,32},{136,40},{144,48},{152,5... | collective-permute-start | bytes 1769480 | tf_op jit(solution)/shard_map/ppermute | solution.py:14
  60.2 66.0 %collective-permute-start.1 = (bf16[384,3,256]{2,0,1:T(8,128)(2,1)}, bf16[384,3,256]{2,0,1:T(8,128)(2,1)}, u32[]{:S(2)}, u32[]{:S(2)}) collective-permute-start(bf16[384,3,256]{2,0,1:T(8,128)(2,1)} %slice.214), channel_id=1, source_target_pairs={{88,0},{96,8},{104,16},{112,24},{120,32},{128,40},{136,48},{144,56... | collective-permute-start | bytes 1769480 | tf_op jit(solution)/shard_map/ppermute | solution.py:14
  62.1 87.5 %collective-permute-start.2 = (bf16[384,3,256]{2,0,1:T(8,128)(2,1)}, bf16[384,3,256]{2,0,1:T(8,128)(2,1)}, u32[]{:S(2)}, u32[]{:S(2)}) collective-permute-start(bf16[384,3,256]{2,0,1:T(8,128)(2,1)} %slice.214), channel_id=1, source_target_pairs={{80,0},{88,8},{96,16},{104,24},{112,32},{120,40},{128,48},{136,56}... | collective-permute-start | bytes 1769480 | tf_op jit(solution)/shard_map/ppermute | solution.py:14
  64.0 100.5 %collective-permute-start.3 = (bf16[384,3,256]{2,0,1:T(8,128)(2,1)}, bf16[384,3,256]{2,0,1:T(8,128)(2,1)}, u32[]{:S(2)}, u32[]{:S(2)}) collective-permute-start(bf16[384,3,256]{2,0,1:T(8,128)(2,1)} %slice.214), channel_id=1, source_target_pairs={{72,0},{80,8},{88,16},{96,24},{104,32},{112,40},{120,48},{128,56},... | collective-permute-start | bytes 1769480 | tf_op jit(solution)/shard_map/ppermute | solution.py:14
  65.9 103.8 %collective-permute-start.4 = (bf16[384,3,256]{2,0,1:T(8,128)(2,1)}, bf16[384,3,256]{2,0,1:T(8,128)(2,1)}, u32[]{:S(2)}, u32[]{:S(2)}) collective-permute-start(bf16[384,3,256]{2,0,1:T(8,128)(2,1)} %slice.214), channel_id=1, source_target_pairs={{64,0},{72,8},{80,16},{88,24},{96,32},{104,40},{112,48},{120,56},{... | collective-permute-start | bytes 1769480 | tf_op jit(solution)/shard_map/ppermute | solution.py:14
  85.6 129.0 %collective-permute-start.5 = (bf16[384,3,256]{2,0,1:T(8,128)(2,1)}, bf16[384,3,256]{2,0,1:T(8,128)(2,1)}, u32[]{:S(2)}, u32[]{:S(2)}) collective-permute-start(bf16[384,3,256]{2,0,1:T(8,128)(2,1)} %slice.214), channel_id=1, source_target_pairs={{56,0},{64,8},{72,16},{80,24},{88,32},{96,40},{104,48},{112,56},{1... | collective-permute-start | bytes 1769480 | tf_op jit(solution)/shard_map/ppermute | solution.py:14
  126.1 90.3 %collective-permute-start.6 = (bf16[384,3,256]{2,0,1:T(8,128)(2,1)}, bf16[384,3,256]{2,0,1:T(8,128)(2,1)}, u32[]{:S(2)}, u32[]{:S(2)}) collective-permute-start(bf16[384,3,256]{2,0,1:T(8,128)(2,1)} %slice.214), channel_id=1, source_target_pairs={{48,0},{56,8},{64,16},{72,24},{80,32},{88,40},{96,48},{104,56},{11... | collective-permute-start | bytes 1769480 | tf_op jit(solution)/shard_map/ppermute | solution.py:14
  149.6 69.4 %collective-permute-start.7 = (bf16[384,3,256]{2,0,1:T(8,128)(2,1)}, bf16[384,3,256]{2,0,1:T(8,128)(2,1)}, u32[]{:S(2)}, u32[]{:S(2)}) collective-permute-start(bf16[384,3,256]{2,0,1:T(8,128)(2,1)} %slice.214), channel_id=1, source_target_pairs={{40,0},{48,8},{56,16},{64,24},{72,32},{80,40},{88,48},{96,56},{104... | collective-permute-start | bytes 1769480 | tf_op jit(solution)/shard_map/ppermute | solution.py:14
  164.5 69.2 %collective-permute-start.8 = (bf16[384,3,256]{2,0,1:T(8,128)(2,1)}, bf16[384,3,256]{2,0,1:T(8,128)(2,1)}, u32[]{:S(2)}, u32[]{:S(2)}) collective-permute-start(bf16[384,3,256]{2,0,1:T(8,128)(2,1)} %slice.214), channel_id=1, source_target_pairs={{32,0},{40,8},{48,16},{56,24},{64,32},{72,40},{80,48},{88,56},{96,... | collective-permute-start | bytes 1769480 | tf_op jit(solution)/shard_map/ppermute | solution.py:14
  169.8 87.0 %collective-permute-start.9 = (bf16[384,3,256]{2,0,1:T(8,128)(2,1)}, bf16[384,3,256]{2,0,1:T(8,128)(2,1)}, u32[]{:S(2)}, u32[]{:S(2)}) collective-permute-start(bf16[384,3,256]{2,0,1:T(8,128)(2,1)} %slice.214), channel_id=1, source_target_pairs={{24,0},{32,8},{40,16},{48,24},{56,32},{64,40},{72,48},{80,56},{88,... | collective-permute-start | bytes 1769480 | tf_op jit(solution)/shard_map/ppermute | solution.py:14
  214.5 70.0 %collective-permute-start.10 = (bf16[384,3,256]{2,0,1:T(8,128)(2,1)}, bf16[384,3,256]{2,0,1:T(8,128)(2,1)}, u32[]{:S(2)}, u32[]{:S(2)}) collective-permute-start(bf16[384,3,256]{2,0,1:T(8,128)(2,1)} %slice.214), channel_id=1, source_target_pairs={{16,0},{24,8},{32,16},{40,24},{48,32},{56,40},{64,48},{72,56},{80,... | collective-permute-start | bytes 1769480 | tf_op jit(solution)/shard_map/ppermute | solution.py:14
  216.5 112.2 %collective-permute-start.11 = (bf16[384,3,256]{2,0,1:T(8,128)(2,1)}, bf16[384,3,256]{2,0,1:T(8,128)(2,1)}, u32[]{:S(2)}, u32[]{:S(2)}) collective-permute-start(bf16[384,3,256]{2,0,1:T(8,128)(2,1)} %slice.214), channel_id=1, source_target_pairs={{8,0},{16,8},{24,16},{32,24},{40,32},{48,40},{56,48},{64,56},{72,6... | collective-permute-start | bytes 1769480 | tf_op jit(solution)/shard_map/ppermute | solution.py:14
  219.0 111.6 %collective-permute-start.12 = (bf16[384,3,256]{2,0,1:T(8,128)(2,1)}, bf16[384,3,256]{2,0,1:T(8,128)(2,1)}, u32[]{:S(2)}, u32[]{:S(2)}) collective-permute-start(bf16[384,3,256]{2,0,1:T(8,128)(2,1)} %slice.214), channel_id=1, source_target_pairs={{0,8},{8,16},{16,24},{24,32},{32,40},{40,48},{48,56},{56,64},{64,7... | collective-permute-start | bytes 1769480 | tf_op jit(solution)/shard_map/ppermute | solution.py:14
  233.6 127.7 %collective-permute-start.13 = (bf16[384,3,256]{2,0,1:T(8,128)(2,1)}, bf16[384,3,256]{2,0,1:T(8,128)(2,1)}, u32[]{:S(2)}, u32[]{:S(2)}) collective-permute-start(bf16[384,3,256]{2,0,1:T(8,128)(2,1)} %slice.214), channel_id=1, source_target_pairs={{0,16},{8,24},{16,32},{24,40},{32,48},{40,56},{48,64},{56,72},{64,... | collective-permute-start | bytes 1769480 | tf_op jit(solution)/shard_map/ppermute | solution.py:14
  256.8 116.2 %collective-permute-start.14 = (bf16[384,3,256]{2,0,1:T(8,128)(2,1)}, bf16[384,3,256]{2,0,1:T(8,128)(2,1)}, u32[]{:S(2)}, u32[]{:S(2)}) collective-permute-start(bf16[384,3,256]{2,0,1:T(8,128)(2,1)} %slice.214), channel_id=1, source_target_pairs={{0,24},{8,32},{16,40},{24,48},{32,56},{40,64},{48,72},{56,80},{64,... | collective-permute-start | bytes 1769480 | tf_op jit(solution)/shard_map/ppermute | solution.py:14
  284.5 90.4 %collective-permute-start.15 = (bf16[384,3,256]{2,0,1:T(8,128)(2,1)}, bf16[384,3,256]{2,0,1:T(8,128)(2,1)}, u32[]{:S(2)}, u32[]{:S(2)}) collective-permute-start(bf16[384,3,256]{2,0,1:T(8,128)(2,1)} %slice.214), channel_id=1, source_target_pairs={{0,32},{8,40},{16,48},{24,56},{32,64},{40,72},{48,80},{56,88},{64,... | collective-permute-start | bytes 1769480 | tf_op jit(solution)/shard_map/ppermute | solution.py:14
  328.6 48.2 %collective-permute-start.16 = (bf16[384,3,256]{2,0,1:T(8,128)(2,1)}, bf16[384,3,256]{2,0,1:T(8,128)(2,1)}, u32[]{:S(2)}, u32[]{:S(2)}) collective-permute-start(bf16[384,3,256]{2,0,1:T(8,128)(2,1)} %slice.214), channel_id=1, source_target_pairs={{0,40},{8,48},{16,56},{24,64},{32,72},{40,80},{48,88},{56,96},{64,... | collective-permute-start | bytes 1769480 | tf_op jit(solution)/shard_map/ppermute | solution.py:14
  330.6 66.9 %collective-permute-start.17 = (bf16[384,3,256]{2,0,1:T(8,128)(2,1)}, bf16[384,3,256]{2,0,1:T(8,128)(2,1)}, u32[]{:S(2)}, u32[]{:S(2)}) collective-permute-start(bf16[384,3,256]{2,0,1:T(8,128)(2,1)} %slice.214), channel_id=1, source_target_pairs={{0,48},{8,56},{16,64},{24,72},{32,80},{40,88},{48,96},{56,104},{64... | collective-permute-start | bytes 1769480 | tf_op jit(solution)/shard_map/ppermute | solution.py:14
  361.3 69.0 %collective-permute-start.18 = (bf16[384,3,256]{2,0,1:T(8,128)(2,1)}, bf16[384,3,256]{2,0,1:T(8,128)(2,1)}, u32[]{:S(2)}, u32[]{:S(2)}) collective-permute-start(bf16[384,3,256]{2,0,1:T(8,128)(2,1)} %slice.214), channel_id=1, source_target_pairs={{0,56},{8,64},{16,72},{24,80},{32,88},{40,96},{48,104},{56,112},{6... | collective-permute-start | bytes 1769480 | tf_op jit(solution)/shard_map/ppermute | solution.py:14
  373.0 208.7 %collective-permute-start.19 = (bf16[384,3,256]{2,0,1:T(8,128)(2,1)}, bf16[384,3,256]{2,0,1:T(8,128)(2,1)}, u32[]{:S(2)}, u32[]{:S(2)}) collective-permute-start(bf16[384,3,256]{2,0,1:T(8,128)(2,1)} %slice.214), channel_id=1, source_target_pairs={{0,64},{8,72},{16,80},{24,88},{32,96},{40,104},{48,112},{56,120},{... | collective-permute-start | bytes 1769480 | tf_op jit(solution)/shard_map/ppermute | solution.py:14
  374.9 212.4 %collective-permute-start.20 = (bf16[384,3,256]{2,0,1:T(8,128)(2,1)}, bf16[384,3,256]{2,0,1:T(8,128)(2,1)}, u32[]{:S(2)}, u32[]{:S(2)}) collective-permute-start(bf16[384,3,256]{2,0,1:T(8,128)(2,1)} %slice.214), channel_id=1, source_target_pairs={{0,72},{8,80},{16,88},{24,96},{32,104},{40,112},{48,120},{56,128},... | collective-permute-start | bytes 1769480 | tf_op jit(solution)/shard_map/ppermute | solution.py:14
  376.9 210.4 %collective-permute-start.21 = (bf16[384,3,256]{2,0,1:T(8,128)(2,1)}, bf16[384,3,256]{2,0,1:T(8,128)(2,1)}, u32[]{:S(2)}, u32[]{:S(2)}) collective-permute-start(bf16[384,3,256]{2,0,1:T(8,128)(2,1)} %slice.214), channel_id=1, source_target_pairs={{0,80},{8,88},{16,96},{24,104},{32,112},{40,120},{48,128},{56,136}... | collective-permute-start | bytes 1769480 | tf_op jit(solution)/shard_map/ppermute | solution.py:14
  397.4 189.9 %collective-permute-start.22 = (bf16[384,3,256]{2,0,1:T(8,128)(2,1)}, bf16[384,3,256]{2,0,1:T(8,128)(2,1)}, u32[]{:S(2)}, u32[]{:S(2)}) collective-permute-start(bf16[384,3,256]{2,0,1:T(8,128)(2,1)} %slice.214), channel_id=1, source_target_pairs={{0,88},{8,96},{16,104},{24,112},{32,120},{40,128},{48,136},{56,144... | collective-permute-start | bytes 1769480 | tf_op jit(solution)/shard_map/ppermute | solution.py:14
  430.4 157.1 %collective-permute-start.23 = (bf16[384,3,256]{2,0,1:T(8,128)(2,1)}, bf16[384,3,256]{2,0,1:T(8,128)(2,1)}, u32[]{:S(2)}, u32[]{:S(2)}) collective-permute-start(bf16[384,3,256]{2,0,1:T(8,128)(2,1)} %slice.214), channel_id=1, source_target_pairs={{0,96},{8,104},{16,112},{24,120},{32,128},{40,136},{48,144},{56,15... | collective-permute-start | bytes 1769480 | tf_op jit(solution)/shard_map/ppermute | solution.py:14
  590.7 59.6 %copy-start.3 = (f32[3072]{0:T(1024)S(1)}, f32[3072]{0:T(1024)}, u32[]{:S(2)}) copy-start(f32[3072]{0:T(1024)} %param.61) | copy-start | bytes 36868
Sparse Core Ops, SparseCore 0:
  590.8 59.3 reduce-scatter.1
